TPU v7x, 512 devices: a whole 4x4x16 slice. The times are simulated.
512 devices in a mesh: dom: 32 (over x, y, z_hi), lat: 16 (over z_lo, core).
Axes of the slice: x: 4, y: 4, z: 16 (z_hi: 2, z_lo: 8; z = z_hi * 8 + z_lo), core: 2. Of those that a mesh axis runs over, the one named last changes fastest.
Arguments:
- states: float32 [3, 64, 256, 1024], P(None, 'dom', 'lat'), may hold values from -3 to 3
- stir_noise: float32 [2, 64, 256, 1024], P(None, 'dom', 'lat'), may hold values from -1.2 to 1.2
- ancestors: int32 [2, 32, 2], replicated, may hold values from 0 to 3, as said below
Outputs:
- filtered: float32 [3, 64, 256, 1024], P(None, 'dom', 'lat')
Inputs may be any that keep to these rules, and one draw needn't show every extreme that they name: An entry from 2 upward names a particle of the preceding island on the loop; in every row ancestors[c, i, :] exactly one entry is 2 or more.
All inputs are finite; a program needn't handle non-finite values.
Results may differ from a plain program's by a relative error of at most 0.0003.
Values sent between devices are 32-bit elements; how exact they have to be, the bound alone decides.
A program may use at most 64 MiB of HBM per device.

v0:
```python
import jax
import jax.numpy as jnp
from jax import lax
from jax.sharding import PartitionSpec as P

STEPS = 2
FILTER_ROUNDS = 2


time_step = 0.2
viscosity = 0.05
rotation = 0.3


def extended(value, sides, width):
    for axis, dim in sides:
        devices, length = (lax.axis_size(axis), value.shape[dim])
        up = [(i, (i + 1) % devices) for i in range(devices - 1)]
        down = [(j, i) for i, j in up]
        last = lax.slice_in_dim(value, length - width, length, axis=dim)
        leading = lax.slice_in_dim(value, 0, width, axis=dim)
        before = lax.ppermute(last, axis, up)
        after = lax.ppermute(leading, axis, down)
        value = jnp.concatenate([before, value, after], axis=dim)
    return value


def shifted(value, axis, steps):
    count = lax.axis_size(axis)
    pairs = [(source, (source + steps) % count) for source in range(count)]
    return lax.ppermute(value, axis, pairs)


def eastward(field_amount):
    return jnp.roll(field_amount, -1, axis=-1)


def westward(field_amount):
    return jnp.roll(field_amount, 1, axis=-1)


def slope_x(field_amount):
    return (eastward(field_amount) - westward(field_amount)) * 0.5


def slope_y(field_amount):
    return (field_amount[..., 2:, :] - field_amount[..., :-2, :]) * 0.5


def laplace(field_amount, middle):
    return (
        eastward(middle)
        + westward(middle)
        + field_amount[..., 2:, :]
        + field_amount[..., :-2, :]
        - 4.0 * middle
    )


def tendency(padded, coriolis):
    height = padded[0]
    zonal = padded[1]
    northward = padded[2]
    height_mid = height[..., 1:-1, :]
    zonal_mid = zonal[..., 1:-1, :]
    north_mid = northward[..., 1:-1, :]
    column_depth = 1.0 + height
    flux_east = column_depth[..., 1:-1, :] * zonal_mid
    flux_north = column_depth * northward
    tend_height = (
        -slope_x(flux_east) - slope_y(flux_north) + viscosity * laplace(height, height_mid)
    )
    tend_zonal = (
        -zonal_mid * slope_x(zonal_mid)
        - north_mid * slope_y(zonal)
        + coriolis * north_mid
        - slope_x(height_mid)
        + viscosity * laplace(zonal, zonal_mid)
    )
    tend_north = (
        -zonal_mid * slope_x(north_mid)
        - north_mid * slope_y(northward)
        - coriolis * zonal_mid
        - slope_y(height)
        + viscosity * laplace(northward, north_mid)
    )
    return jnp.stack([tend_height, tend_zonal, tend_north])


def coriolis_rows(start_row, row_count, all_rows):
    row_index = start_row + jnp.arange(row_count, dtype=jnp.int32)
    return (rotation * (2.0 * (row_index.astype(jnp.float32) + 0.5) / all_rows - 1.0))[:, None]


def rim_single(fields):
    return extended(fields, (("lat", 2),), 1)


def choose(candidates, wanted):
    result = candidates[:, 0]
    for source_slot in range(1, candidates.shape[1]):
        result = jnp.where(wanted == source_slot, candidates[:, source_slot], result)
    return result


def body(states, stir_noise, ancestors):
    per_island = states.shape[1]
    local_rows = states.shape[2]
    total_rows = local_rows * lax.axis_size("lat")
    first_row = lax.axis_index("lat") * local_rows
    island = lax.axis_index("dom")
    coriolis_here = coriolis_rows(first_row, local_rows, total_rows)
    fields = states
    for cycle_idx in range(FILTER_ROUNDS):
        for step_idx in range(STEPS):
            padded = rim_single(fields)
            first_section = fields + time_step * tendency(padded, coriolis_here)
            padded_section = rim_single(first_section)
            fields = 0.5 * (
                fields
                + padded_section[..., 1:-1, :]
                + time_step * tendency(padded_section, coriolis_here)
            )
        fields = jnp.concatenate([fields[0:1] + stir_noise[cycle_idx][None], fields[1:]], axis=0)
        cycle_parents = ancestors[cycle_idx]
        parent_row = lax.dynamic_index_in_dim(cycle_parents, island, 0, keepdims=False)
        arrived = shifted(fields, "dom", 1)
        candidates = jnp.concatenate([fields, arrived], axis=1)
        fields = jnp.stack(
            [choose(candidates, parent_row[target_slot]) for target_slot in range(per_island)],
            axis=1,
        )
    return fields


def solution(mesh):
    in_specs = (P(None, "dom", "lat", None), P(None, "dom", "lat", None), P())
    out_specs = P(None, "dom", "lat", None)
    return jax.shard_map(body, mesh=mesh, in_specs=in_specs, out_specs=out_specs, check_vma=False)
```

profile of v0, /device:TPU:103, one launch (start us, length us, event | category | flops | bytes accessed | tf_op | source)
XLA Modules:
  0.0 177.0 jit_solution(10786872615512607472)
XLA Ops:
  0.0 1.1 fusion.96
  1.1 2.6 %collective-permute-start.1 = (f32[3,2,1,1024]{3,2,1,0:T(1,128)S(1)}, f32[3,2,1,1024]{3,2,1,0:T(1,128)S(1)}, u32[]{:S(2)}, u32[]{:S(2)}) collective-permute-start(f32[3,2,1,1024]{3,2,1,0:T(1,128)S(1)} %get-tuple-element.64), channel_id=1, source_target_pairs={{1,0},{2,1},{3,2},{4,3},{5,4},{6,5},{7,6},{8,7},{9,8},{10,9},{11,1... | collective-permute-start | bytes 73736 | tf_op jit(solution)/shard_map/ppermute | solution.py:23
  3.7 4.7 %collective-permute-start = (f32[3,2,1,1024]{3,2,1,0:T(1,128)S(1)}, f32[3,2,1,1024]{3,2,1,0:T(1,128)S(1)}, u32[]{:S(2)}, u32[]{:S(2)}) collective-permute-start(f32[3,2,1,1024]{3,2,1,0:T(1,128)S(1)} %get-tuple-element.63), channel_id=1, source_target_pairs={{0,1},{1,2},{2,3},{3,4},{4,5},{5,6},{6,7},{7,8},{8,9},{9,10},{10,1... | collective-permute-start | bytes 73736 | tf_op jit(solution)/shard_map/ppermute | solution.py:22
  8.3 0.9 collective-permute-done
  9.2 1.1 pad_maximum_fusion.2
  10.8 0.2 slice_multiply_fusion.15
  11.2 0.2 add_bitcast_fusion.15
  11.6 0.8 copy-done
  12.5 1.9 %collective-permute-start.3 = (f32[3,2,1,1024]{3,2,1,0:T(1,128)S(1)}, f32[3,2,1,1024]{3,2,1,0:T(1,128)S(1)}, u32[]{:S(2)}, u32[]{:S(2)}) collective-permute-start(f32[3,2,1,1024]{3,2,1,0:T(1,128)S(1)} %get-tuple-element.62), channel_id=1, source_target_pairs={{1,0},{2,1},{3,2},{4,3},{5,4},{6,5},{7,6},{8,7},{9,8},{10,9},{11,1... | collective-permute-start | bytes 73736 | tf_op jit(solution)/shard_map/ppermute | solution.py:23
  14.4 5.4 %collective-permute-start.2 = (f32[3,2,1,1024]{3,2,1,0:T(1,128)S(1)}, f32[3,2,1,1024]{3,2,1,0:T(1,128)S(1)}, u32[]{:S(2)}, u32[]{:S(2)}) collective-permute-start(f32[3,2,1,1024]{3,2,1,0:T(1,128)S(1)} %get-tuple-element.61), channel_id=1, source_target_pairs={{0,1},{1,2},{2,3},{3,4},{4,5},{5,6},{6,7},{7,8},{8,9},{9,10},{10,1... | collective-permute-start | bytes 73736 | tf_op jit(solution)/shard_map/ppermute | solution.py:22
  19.9 0.9 collective-permute-done.2
  21.5 0.2 slice_multiply_fusion.13
  22.4 1.9 %collective-permute-start.5 = (f32[3,2,1,1024]{3,2,1,0:T(1,128)S(1)}, f32[3,2,1,1024]{3,2,1,0:T(1,128)S(1)}, u32[]{:S(2)}, u32[]{:S(2)}) collective-permute-start(f32[3,2,1,1024]{3,2,1,0:T(1,128)S(1)} %get-tuple-element.60), channel_id=1, source_target_pairs={{1,0},{2,1},{3,2},{4,3},{5,4},{6,5},{7,6},{8,7},{9,8},{10,9},{11,1... | collective-permute-start | bytes 73736 | tf_op jit(solution)/shard_map/ppermute | solution.py:23
  24.3 5.4 %collective-permute-start.4 = (f32[3,2,1,1024]{3,2,1,0:T(1,128)S(1)}, f32[3,2,1,1024]{3,2,1,0:T(1,128)S(1)}, u32[]{:S(2)}, u32[]{:S(2)}) collective-permute-start(f32[3,2,1,1024]{3,2,1,0:T(1,128)S(1)} %get-tuple-element.59), channel_id=1, source_target_pairs={{0,1},{1,2},{2,3},{3,4},{4,5},{5,6},{6,7},{7,8},{8,9},{9,10},{10,1... | collective-permute-start | bytes 73736 | tf_op jit(solution)/shard_map/ppermute | solution.py:22
  29.8 0.9 collective-permute-done.4
  31.4 0.2 slice_multiply_fusion.11
  32.3 1.9 %collective-permute-start.7 = (f32[3,2,1,1024]{3,2,1,0:T(1,128)S(1)}, f32[3,2,1,1024]{3,2,1,0:T(1,128)S(1)}, u32[]{:S(2)}, u32[]{:S(2)}) collective-permute-start(f32[3,2,1,1024]{3,2,1,0:T(1,128)S(1)} %get-tuple-element.58), channel_id=1, source_target_pairs={{1,0},{2,1},{3,2},{4,3},{5,4},{6,5},{7,6},{8,7},{9,8},{10,9},{11,1... | collective-permute-start | bytes 73736 | tf_op jit(solution)/shard_map/ppermute | solution.py:23
  34.3 5.4 %collective-permute-start.6 = (f32[3,2,1,1024]{3,2,1,0:T(1,128)S(1)}, f32[3,2,1,1024]{3,2,1,0:T(1,128)S(1)}, u32[]{:S(2)}, u32[]{:S(2)}) collective-permute-start(f32[3,2,1,1024]{3,2,1,0:T(1,128)S(1)} %get-tuple-element.57), channel_id=1, source_target_pairs={{0,1},{1,2},{2,3},{3,4},{4,5},{5,6},{6,7},{7,8},{8,9},{9,10},{10,1... | collective-permute-start | bytes 73736 | tf_op jit(solution)/shard_map/ppermute | solution.py:22
  39.7 0.9 collective-permute-done.6
  41.3 0.2 slice_multiply_fusion.9
  41.7 0.2 add_bitcast_fusion.9
  42.1 0.2 fusion.5
  42.3 0.9 copy-done.1
  43.3 12.3 %collective-permute-start.8 = (f32[3,2,16,1024]{3,2,1,0:T(8,128)S(1)}, f32[3,2,16,1024]{3,2,1,0:T(8,128)S(1)}, u32[]{:S(2)}, u32[]{:S(2)}) collective-permute-start(f32[3,2,16,1024]{3,2,1,0:T(8,128)S(1)} %pad_maximum_fusion), channel_id=1, source_target_pairs={{0,16},{16,32},{32,48},{48,64},{64,80},{80,96},{96,112},{112,128},... | collective-permute-start | bytes 1179656 | tf_op jit(solution)/shard_map/ppermute | solution.py:31
  55.7 0.6 fusion.163
  60.1 30.6 %collective-permute-done.8 = f32[3,2,16,1024]{3,2,1,0:T(8,128)S(1)} collective-permute-done((f32[3,2,16,1024]{3,2,1,0:T(8,128)S(1)}, f32[3,2,16,1024]{3,2,1,0:T(8,128)S(1)}, u32[]{:S(2)}, u32[]{:S(2)}) %collective-permute-start.8) | collective-permute-done | bytes 393248 | tf_op jit(solution)/shard_map/ppermute | solution.py:31
  90.8 1.9 %collective-permute-start.10 = (f32[3,2,1,1024]{3,2,1,0:T(1,128)S(1)}, f32[3,2,1,1024]{3,2,1,0:T(1,128)S(1)}, u32[]{:S(2)}, u32[]{:S(2)}) collective-permute-start(f32[3,2,1,1024]{3,2,1,0:T(1,128)S(1)} %get-tuple-element.56), channel_id=1, source_target_pairs={{1,0},{2,1},{3,2},{4,3},{5,4},{6,5},{7,6},{8,7},{9,8},{10,9},{11,1... | collective-permute-start | bytes 73736 | tf_op jit(solution)/shard_map/ppermute | solution.py:23
  92.7 4.9 %collective-permute-start.9 = (f32[3,2,1,1024]{3,2,1,0:T(1,128)S(1)}, f32[3,2,1,1024]{3,2,1,0:T(1,128)S(1)}, u32[]{:S(2)}, u32[]{:S(2)}) collective-permute-start(f32[3,2,1,1024]{3,2,1,0:T(1,128)S(1)} %get-tuple-element.55), channel_id=1, source_target_pairs={{0,1},{1,2},{2,3},{3,4},{4,5},{5,6},{6,7},{7,8},{8,9},{9,10},{10,1... | collective-permute-start | bytes 73736 | tf_op jit(solution)/shard_map/ppermute | solution.py:22
  97.6 0.9 collective-permute-done.9
  99.2 0.2 slice_multiply_fusion.7
  99.6 0.2 add_bitcast_fusion.7
  100.0 1.9 %collective-permute-start.12 = (f32[3,2,1,1024]{3,2,1,0:T(1,128)S(1)}, f32[3,2,1,1024]{3,2,1,0:T(1,128)S(1)}, u32[]{:S(2)}, u32[]{:S(2)}) collective-permute-start(f32[3,2,1,1024]{3,2,1,0:T(1,128)S(1)} %get-tuple-element.54), channel_id=1, source_target_pairs={{1,0},{2,1},{3,2},{4,3},{5,4},{6,5},{7,6},{8,7},{9,8},{10,9},{11,1... | collective-permute-start | bytes 73736 | tf_op jit(solution)/shard_map/ppermute | solution.py:23
  102.0 5.4 %collective-permute-start.11 = (f32[3,2,1,1024]{3,2,1,0:T(1,128)S(1)}, f32[3,2,1,1024]{3,2,1,0:T(1,128)S(1)}, u32[]{:S(2)}, u32[]{:S(2)}) collective-permute-start(f32[3,2,1,1024]{3,2,1,0:T(1,128)S(1)} %get-tuple-element.53), channel_id=1, source_target_pairs={{0,1},{1,2},{2,3},{3,4},{4,5},{5,6},{6,7},{7,8},{8,9},{9,10},{10,1... | collective-permute-start | bytes 73736 | tf_op jit(solution)/shard_map/ppermute | solution.py:22
  107.4 0.9 collective-permute-done.11
  109.0 0.2 slice_multiply_fusion.5
  109.9 1.9 %collective-permute-start.14 = (f32[3,2,1,1024]{3,2,1,0:T(1,128)S(1)}, f32[3,2,1,1024]{3,2,1,0:T(1,128)S(1)}, u32[]{:S(2)}, u32[]{:S(2)}) collective-permute-start(f32[3,2,1,1024]{3,2,1,0:T(1,128)S(1)} %get-tuple-element.52), channel_id=1, source_target_pairs={{1,0},{2,1},{3,2},{4,3},{5,4},{6,5},{7,6},{8,7},{9,8},{10,9},{11,1... | collective-permute-start | bytes 73736 | tf_op jit(solution)/shard_map/ppermute | solution.py:23
  111.9 5.4 %collective-permute-start.13 = (f32[3,2,1,1024]{3,2,1,0:T(1,128)S(1)}, f32[3,2,1,1024]{3,2,1,0:T(1,128)S(1)}, u32[]{:S(2)}, u32[]{:S(2)}) collective-permute-start(f32[3,2,1,1024]{3,2,1,0:T(1,128)S(1)} %get-tuple-element.51), channel_id=1, source_target_pairs={{0,1},{1,2},{2,3},{3,4},{4,5},{5,6},{6,7},{7,8},{8,9},{9,10},{10,1... | collective-permute-start | bytes 73736 | tf_op jit(solution)/shard_map/ppermute | solution.py:22
  117.3 0.9 collective-permute-done.13
  118.9 0.2 slice_multiply_fusion.3
  119.9 1.9 %collective-permute-start.16 = (f32[3,2,1,1024]{3,2,1,0:T(1,128)S(1)}, f32[3,2,1,1024]{3,2,1,0:T(1,128)S(1)}, u32[]{:S(2)}, u32[]{:S(2)}) collective-permute-start(f32[3,2,1,1024]{3,2,1,0:T(1,128)S(1)} %get-tuple-element.50), channel_id=1, source_target_pairs={{1,0},{2,1},{3,2},{4,3},{5,4},{6,5},{7,6},{8,7},{9,8},{10,9},{11,1... | collective-permute-start | bytes 73736 | tf_op jit(solution)/shard_map/ppermute | solution.py:23
  121.8 5.4 %collective-permute-start.15 = (f32[3,2,1,1024]{3,2,1,0:T(1,128)S(1)}, f32[3,2,1,1024]{3,2,1,0:T(1,128)S(1)}, u32[]{:S(2)}, u32[]{:S(2)}) collective-permute-start(f32[3,2,1,1024]{3,2,1,0:T(1,128)S(1)} %get-tuple-element.49), channel_id=1, source_target_pairs={{0,1},{1,2},{2,3},{3,4},{4,5},{5,6},{6,7},{7,8},{8,9},{9,10},{10,1... | collective-permute-start | bytes 73736 | tf_op jit(solution)/shard_map/ppermute | solution.py:22
  127.2 0.9 collective-permute-done.15
  128.9 0.2 slice_multiply_fusion.1
  129.6 0.2 fusion.11
  129.9 7.4 %collective-permute-start.17 = (f32[3,2,16,1024]{3,2,1,0:T(8,128)S(1)}, f32[3,2,16,1024]{3,2,1,0:T(8,128)S(1)}, u32[]{:S(2)}, u32[]{:S(2)}) collective-permute-start(f32[3,2,16,1024]{3,2,1,0:T(8,128)S(1)} %pad_maximum_fusion.1), channel_id=1, source_target_pairs={{0,16},{16,32},{32,48},{48,64},{64,80},{80,96},{96,112},{112,128},... | collective-permute-start | bytes 1179656 | tf_op jit(solution)/shard_map/ppermute | solution.py:31
  137.3 0.6 fusion.162
  141.7 34.5 %collective-permute-done.17 = f32[3,2,16,1024]{3,2,1,0:T(8,128)S(1)} collective-permute-done((f32[3,2,16,1024]{3,2,1,0:T(8,128)S(1)}, f32[3,2,16,1024]{3,2,1,0:T(8,128)S(1)}, u32[]{:S(2)}, u32[]{:S(2)}) %collective-permute-start.17) | collective-permute-done | bytes 393248 | tf_op jit(solution)/shard_map/ppermute | solution.py:31
  176.3 0.8 pad_maximum_fusion.11
  (134 shorter events, 9.8 us)
Async XLA Ops:
  1.1 7.3 %collective-permute-start.1 = (f32[3,2,1,1024]{3,2,1,0:T(1,128)S(1)}, f32[3,2,1,1024]{3,2,1,0:T(1,128)S(1)}, u32[]{:S(2)}, u32[]{:S(2)}) collective-permute-start(f32[3,2,1,1024]{3,2,1,0:T(1,128)S(1)} %get-tuple-element.64), channel_id=1, source_target_pairs={{1,0},{2,1},{3,2},{4,3},{5,4},{6,5},{7,6},{8,7},{9,8},{10,9},{11,1... | collective-permute-start | bytes 73736 | tf_op jit(solution)/shard_map/ppermute | solution.py:23
  3.7 5.6 %collective-permute-start = (f32[3,2,1,1024]{3,2,1,0:T(1,128)S(1)}, f32[3,2,1,1024]{3,2,1,0:T(1,128)S(1)}, u32[]{:S(2)}, u32[]{:S(2)}) collective-permute-start(f32[3,2,1,1024]{3,2,1,0:T(1,128)S(1)} %get-tuple-element.63), channel_id=1, source_target_pairs={{0,1},{1,2},{2,3},{3,4},{4,5},{5,6},{6,7},{7,8},{8,9},{9,10},{10,1... | collective-permute-start | bytes 73736 | tf_op jit(solution)/shard_map/ppermute | solution.py:22
  11.4 1.0 copy-start
  12.5 7.4 %collective-permute-start.3 = (f32[3,2,1,1024]{3,2,1,0:T(1,128)S(1)}, f32[3,2,1,1024]{3,2,1,0:T(1,128)S(1)}, u32[]{:S(2)}, u32[]{:S(2)}) collective-permute-start(f32[3,2,1,1024]{3,2,1,0:T(1,128)S(1)} %get-tuple-element.62), channel_id=1, source_target_pairs={{1,0},{2,1},{3,2},{4,3},{5,4},{6,5},{7,6},{8,7},{9,8},{10,9},{11,1... | collective-permute-start | bytes 73736 | tf_op jit(solution)/shard_map/ppermute | solution.py:23
  14.4 6.4 %collective-permute-start.2 = (f32[3,2,1,1024]{3,2,1,0:T(1,128)S(1)}, f32[3,2,1,1024]{3,2,1,0:T(1,128)S(1)}, u32[]{:S(2)}, u32[]{:S(2)}) collective-permute-start(f32[3,2,1,1024]{3,2,1,0:T(1,128)S(1)} %get-tuple-element.61), channel_id=1, source_target_pairs={{0,1},{1,2},{2,3},{3,4},{4,5},{5,6},{6,7},{7,8},{8,9},{9,10},{10,1... | collective-permute-start | bytes 73736 | tf_op jit(solution)/shard_map/ppermute | solution.py:22
  22.4 7.4 %collective-permute-start.5 = (f32[3,2,1,1024]{3,2,1,0:T(1,128)S(1)}, f32[3,2,1,1024]{3,2,1,0:T(1,128)S(1)}, u32[]{:S(2)}, u32[]{:S(2)}) collective-permute-start(f32[3,2,1,1024]{3,2,1,0:T(1,128)S(1)} %get-tuple-element.60), channel_id=1, source_target_pairs={{1,0},{2,1},{3,2},{4,3},{5,4},{6,5},{7,6},{8,7},{9,8},{10,9},{11,1... | collective-permute-start | bytes 73736 | tf_op jit(solution)/shard_map/ppermute | solution.py:23
  24.3 6.4 %collective-permute-start.4 = (f32[3,2,1,1024]{3,2,1,0:T(1,128)S(1)}, f32[3,2,1,1024]{3,2,1,0:T(1,128)S(1)}, u32[]{:S(2)}, u32[]{:S(2)}) collective-permute-start(f32[3,2,1,1024]{3,2,1,0:T(1,128)S(1)} %get-tuple-element.59), channel_id=1, source_target_pairs={{0,1},{1,2},{2,3},{3,4},{4,5},{5,6},{6,7},{7,8},{8,9},{9,10},{10,1... | collective-permute-start | bytes 73736 | tf_op jit(solution)/shard_map/ppermute | solution.py:22
  32.3 7.4 %collective-permute-start.7 = (f32[3,2,1,1024]{3,2,1,0:T(1,128)S(1)}, f32[3,2,1,1024]{3,2,1,0:T(1,128)S(1)}, u32[]{:S(2)}, u32[]{:S(2)}) collective-permute-start(f32[3,2,1,1024]{3,2,1,0:T(1,128)S(1)} %get-tuple-element.58), channel_id=1, source_target_pairs={{1,0},{2,1},{3,2},{4,3},{5,4},{6,5},{7,6},{8,7},{9,8},{10,9},{11,1... | collective-permute-start | bytes 73736 | tf_op jit(solution)/shard_map/ppermute | solution.py:23
  34.3 6.4 %collective-permute-start.6 = (f32[3,2,1,1024]{3,2,1,0:T(1,128)S(1)}, f32[3,2,1,1024]{3,2,1,0:T(1,128)S(1)}, u32[]{:S(2)}, u32[]{:S(2)}) collective-permute-start(f32[3,2,1,1024]{3,2,1,0:T(1,128)S(1)} %get-tuple-element.57), channel_id=1, source_target_pairs={{0,1},{1,2},{2,3},{3,4},{4,5},{5,6},{6,7},{7,8},{8,9},{9,10},{10,1... | collective-permute-start | bytes 73736 | tf_op jit(solution)/shard_map/ppermute | solution.py:22
  42.3 1.0 copy-start.1
  43.3 12.3 %copy-start.2 = (s32[2,32,2]{1,2,0:T(2,128)S(1)}, s32[2,32,2]{1,2,0:T(2,128)}, u32[]{:S(2)}) copy-start(s32[2,32,2]{1,2,0:T(2,128)} %param.5) | copy-start | bytes 1540
  43.3 47.4 %collective-permute-start.8 = (f32[3,2,16,1024]{3,2,1,0:T(8,128)S(1)}, f32[3,2,16,1024]{3,2,1,0:T(8,128)S(1)}, u32[]{:S(2)}, u32[]{:S(2)}) collective-permute-start(f32[3,2,16,1024]{3,2,1,0:T(8,128)S(1)} %pad_maximum_fusion), channel_id=1, source_target_pairs={{0,16},{16,32},{32,48},{48,64},{64,80},{80,96},{96,112},{112,128},... | collective-permute-start | bytes 1179656 | tf_op jit(solution)/shard_map/ppermute | solution.py:31
  90.8 6.8 %collective-permute-start.10 = (f32[3,2,1,1024]{3,2,1,0:T(1,128)S(1)}, f32[3,2,1,1024]{3,2,1,0:T(1,128)S(1)}, u32[]{:S(2)}, u32[]{:S(2)}) collective-permute-start(f32[3,2,1,1024]{3,2,1,0:T(1,128)S(1)} %get-tuple-element.56), channel_id=1, source_target_pairs={{1,0},{2,1},{3,2},{4,3},{5,4},{6,5},{7,6},{8,7},{9,8},{10,9},{11,1... | collective-permute-start | bytes 73736 | tf_op jit(solution)/shard_map/ppermute | solution.py:23
  92.7 5.8 %collective-permute-start.9 = (f32[3,2,1,1024]{3,2,1,0:T(1,128)S(1)}, f32[3,2,1,1024]{3,2,1,0:T(1,128)S(1)}, u32[]{:S(2)}, u32[]{:S(2)}) collective-permute-start(f32[3,2,1,1024]{3,2,1,0:T(1,128)S(1)} %get-tuple-element.55), channel_id=1, source_target_pairs={{0,1},{1,2},{2,3},{3,4},{4,5},{5,6},{6,7},{7,8},{8,9},{9,10},{10,1... | collective-permute-start | bytes 73736 | tf_op jit(solution)/shard_map/ppermute | solution.py:22
  100.0 7.4 %collective-permute-start.12 = (f32[3,2,1,1024]{3,2,1,0:T(1,128)S(1)}, f32[3,2,1,1024]{3,2,1,0:T(1,128)S(1)}, u32[]{:S(2)}, u32[]{:S(2)}) collective-permute-start(f32[3,2,1,1024]{3,2,1,0:T(1,128)S(1)} %get-tuple-element.54), channel_id=1, source_target_pairs={{1,0},{2,1},{3,2},{4,3},{5,4},{6,5},{7,6},{8,7},{9,8},{10,9},{11,1... | collective-permute-start | bytes 73736 | tf_op jit(solution)/shard_map/ppermute | solution.py:23
  102.0 6.4 %collective-permute-start.11 = (f32[3,2,1,1024]{3,2,1,0:T(1,128)S(1)}, f32[3,2,1,1024]{3,2,1,0:T(1,128)S(1)}, u32[]{:S(2)}, u32[]{:S(2)}) collective-permute-start(f32[3,2,1,1024]{3,2,1,0:T(1,128)S(1)} %get-tuple-element.53), channel_id=1, source_target_pairs={{0,1},{1,2},{2,3},{3,4},{4,5},{5,6},{6,7},{7,8},{8,9},{9,10},{10,1... | collective-permute-start | bytes 73736 | tf_op jit(solution)/shard_map/ppermute | solution.py:22
  109.9 7.4 %collective-permute-start.14 = (f32[3,2,1,1024]{3,2,1,0:T(1,128)S(1)}, f32[3,2,1,1024]{3,2,1,0:T(1,128)S(1)}, u32[]{:S(2)}, u32[]{:S(2)}) collective-permute-start(f32[3,2,1,1024]{3,2,1,0:T(1,128)S(1)} %get-tuple-element.52), channel_id=1, source_target_pairs={{1,0},{2,1},{3,2},{4,3},{5,4},{6,5},{7,6},{8,7},{9,8},{10,9},{11,1... | collective-permute-start | bytes 73736 | tf_op jit(solution)/shard_map/ppermute | solution.py:23
  111.9 6.4 %collective-permute-start.13 = (f32[3,2,1,1024]{3,2,1,0:T(1,128)S(1)}, f32[3,2,1,1024]{3,2,1,0:T(1,128)S(1)}, u32[]{:S(2)}, u32[]{:S(2)}) collective-permute-start(f32[3,2,1,1024]{3,2,1,0:T(1,128)S(1)} %get-tuple-element.51), channel_id=1, source_target_pairs={{0,1},{1,2},{2,3},{3,4},{4,5},{5,6},{6,7},{7,8},{8,9},{9,10},{10,1... | collective-permute-start | bytes 73736 | tf_op jit(solution)/shard_map/ppermute | solution.py:22
  119.9 7.4 %collective-permute-start.16 = (f32[3,2,1,1024]{3,2,1,0:T(1,128)S(1)}, f32[3,2,1,1024]{3,2,1,0:T(1,128)S(1)}, u32[]{:S(2)}, u32[]{:S(2)}) collective-permute-start(f32[3,2,1,1024]{3,2,1,0:T(1,128)S(1)} %get-tuple-element.50), channel_id=1, source_target_pairs={{1,0},{2,1},{3,2},{4,3},{5,4},{6,5},{7,6},{8,7},{9,8},{10,9},{11,1... | collective-permute-start | bytes 73736 | tf_op jit(solution)/shard_map/ppermute | solution.py:23
  121.8 6.4 %collective-permute-start.15 = (f32[3,2,1,1024]{3,2,1,0:T(1,128)S(1)}, f32[3,2,1,1024]{3,2,1,0:T(1,128)S(1)}, u32[]{:S(2)}, u32[]{:S(2)}) collective-permute-start(f32[3,2,1,1024]{3,2,1,0:T(1,128)S(1)} %get-tuple-element.49), channel_id=1, source_target_pairs={{0,1},{1,2},{2,3},{3,4},{4,5},{5,6},{6,7},{7,8},{8,9},{9,10},{10,1... | collective-permute-start | bytes 73736 | tf_op jit(solution)/shard_map/ppermute | solution.py:22
  129.9 46.3 %collective-permute-start.17 = (f32[3,2,16,1024]{3,2,1,0:T(8,128)S(1)}, f32[3,2,16,1024]{3,2,1,0:T(8,128)S(1)}, u32[]{:S(2)}, u32[]{:S(2)}) collective-permute-start(f32[3,2,16,1024]{3,2,1,0:T(8,128)S(1)} %pad_maximum_fusion.1), channel_id=1, source_target_pairs={{0,16},{16,32},{32,48},{48,64},{64,80},{80,96},{96,112},{112,128},... | collective-permute-start | bytes 1179656 | tf_op jit(solution)/shard_map/ppermute | solution.py:31
where the time goes:
time: 178 us; the launch traced here: 177 us
  starting transfers between devices  77.7 us (44%)
  waiting for transfers between devices  72.4 us (41%)
  local copies, waits for them, and re-layouts  9.93 us (6%)
  between operations  8.67 us (5%)
  other arithmetic  8.28 us (5%)
    ppermute x2, waiting for transfers between devices, shifted(): return lax.ppermute(value, axis, pairs)  65.1 us
    ppermute x8, starting transfers between devices, extended(): before = lax.ppermute(last, axis, up)  42.1 us
    ppermute x2, starting transfers between devices, shifted(): return lax.ppermute(value, axis, pairs)  19.7 us
    ppermute x8, starting transfers between devices, extended(): after = lax.ppermute(leading, axis, down)  16 us
    ppermute x8, waiting for transfers between devices, extended(): before = lax.ppermute(last, axis, up)  7.29 us
    slice x46, local copies, waits for them, and re-layouts, eastward(): return jnp.roll(field_amount, -1, axis=-1)  3.97 us
  transfers between devices with their start and end apart: 18, of which 10 were waited for; matrix products, arithmetic and copies ran while one was open for 1% of the time, Pallas kernels for 0%

commit v1 on v0

v1 whole, which is shorter than its diff:
```python
import functools

import jax
import jax.numpy as jnp
from jax import lax
from jax.experimental import pallas as pl
from jax.experimental.pallas import tpu as pltpu
from jax.sharding import PartitionSpec as P

MESH = pl.DeviceIdType.MESH
DT = 0.2
HALF = 0.5 * DT
NU = 0.05 * DT
ROT = 0.3
W = 1024
HOPS = 8


def terms(h, u, v, hs, us, vs, cor):
    he, hw, hn, hb = hs
    ue, uw, un, ub = us
    ve, vw, vn, vb = vs
    dux = ue - uw
    dvy = vn - vb
    bh = (he * ue - hw * uw) + (hn * vn - hb * vb) + (dux + dvy)
    bu = u * dux + v * (un - ub) + (he - hw)
    bv = u * (ve - vw) + v * dvy + (hn - hb)
    lh = (he + hw) + (hn + hb)
    lu = (ue + uw) + (un + ub)
    lv = (ve + vw) + (vn + vb)
    keep = 1.0 - 4.0 * NU
    return (
        h * keep + NU * lh - HALF * bh,
        u * keep + NU * lu - HALF * bu + cor * v,
        v * keep + NU * lv - HALF * bv - cor * u,
    )


def stage_tile(src, old, cor, t):
    r = 8 * t
    sub = lax.broadcasted_iota(jnp.int32, (8, W), 0)
    mid, shifts = [], []
    for f in range(3):
        c = src[f, pl.ds(r, 8), :]
        nxt = src[f, pl.ds(r + 8, 8), :]
        prv = src[f, pl.ds(r - 8, 8), :]
        mid.append(c)
        shifts.append(
            (
                pltpu.roll(c, W - 1, 1),
                pltpu.roll(c, 1, 1),
                jnp.where(sub == 7, pltpu.roll(nxt, 7, 0), pltpu.roll(c, 7, 0)),
                jnp.where(sub == 0, pltpu.roll(prv, 1, 0), pltpu.roll(c, 1, 0)),
            )
        )
    cr = jnp.broadcast_to(cor[pl.ds(r, 8), 0:1], (8, W))
    new = terms(*mid, *shifts, cr)
    if old is None:
        return new
    return tuple(0.5 * (old[f, pl.ds(r, 8), :] + new[f]) for f in range(3))


def kernel(
    islands, lats, anc, states, noise, out, xe, ne, n1, a, b, cor, own, foh, ring, byp, ovm,
    lsem, hsend, hrecv, rsend, rrecv, bsend, brecv, osem,
):
    dom, lat = lax.axis_index("dom"), lax.axis_index("lat")
    columns = islands // 2
    half = lats // 2
    depth = 2 * half
    xy, core = dom // 2, lat % 2
    z = (dom % 2) * half + lat // 2

    def at(xy_, z_):
        return (xy_ * 2 + z_ // half, (z_ % half) * 2 + core)

    zs = ((z + 1) % depth, (z + depth - 1) % depth)
    nxt_xy, prv_xy = (xy + 1) % columns, (xy + columns - 1) % columns
    low = (z < half).astype(jnp.int32)

    def hop(d, n):
        zt = zs[d]
        if n < HOPS:
            return at(xy, zt)
        return at((xy + (zt < half).astype(jnp.int32)) % columns, zt)

    loads = [
        pltpu.make_async_copy(states, xe.at[:, :, pl.ds(8, 16)], lsem.at[0]),
        pltpu.make_async_copy(noise.at[0], ne.at[:, pl.ds(8, 16)], lsem.at[1]),
        pltpu.make_async_copy(noise.at[1], n1, lsem.at[2]),
    ]
    for c in loads:
        c.start()

    barrier = pltpu.get_barrier_semaphore()
    from_xy = (xy + columns - low) % columns
    for d in range(2):
        pl.semaphore_signal(barrier, 1, device_id=at(xy, zs[d]), device_id_type=MESH)
        pl.semaphore_signal(barrier, 1, device_id=at(from_xy, zs[d]), device_id_type=MESH)
    pl.semaphore_signal(barrier, 1, device_id=at(prv_xy, z), device_id_type=MESH)

    @pl.when(lat > 0)
    def _():
        pl.semaphore_signal(barrier, 1, device_id=(dom, lat - 1), device_id_type=MESH)

    @pl.when(lat < lats - 1)
    def _():
        pl.semaphore_signal(barrier, 1, device_id=(dom, lat + 1), device_id_type=MESH)

    row = lax.broadcasted_iota(jnp.int32, (48, 128), 0) - 16 + lat * 16
    cor[...] = (DT * ROT) * (2.0 * (row.astype(jnp.float32) + 0.5) / (lats * 16) - 1.0)

    @pl.when(lat == 0)
    def _():
        xe[:, :, pl.ds(0, 8), :] = jnp.zeros((3, 2, 8, W), jnp.float32)
        ne[:, pl.ds(0, 8), :] = jnp.zeros((2, 8, W), jnp.float32)

    @pl.when(lat == lats - 1)
    def _():
        xe[:, :, pl.ds(24, 8), :] = jnp.zeros((3, 2, 8, W), jnp.float32)
        ne[:, pl.ds(24, 8), :] = jnp.zeros((2, 8, W), jnp.float32)

    for c in loads:
        c.wait()
    pl.semaphore_wait(
        barrier, 5 + (lat > 0).astype(jnp.int32) + (lat < lats - 1).astype(jnp.int32)
    )

    def halo(d):
        s, t = (8, 24) if d == 0 else (16, 0)
        dev = (dom, lat - 1) if d == 0 else (dom, lat + 1)
        return [
            pltpu.make_async_remote_copy(
                xe.at[:, :, pl.ds(s, 8)], xe.at[:, :, pl.ds(t, 8)], hsend.at[d, 0], hrecv.at[d, 0],
                device_id=dev, device_id_type=MESH,
            ),
            pltpu.make_async_remote_copy(
                ne.at[:, pl.ds(s, 8)], ne.at[:, pl.ds(t, 8)], hsend.at[d, 1], hrecv.at[d, 1],
                device_id=dev, device_id_type=MESH,
            ),
        ]

    @pl.when(lat > 0)
    def _():
        for c in halo(0):
            c.start()

    @pl.when(lat < lats - 1)
    def _():
        for c in halo(1):
            c.start()

    def row_of(c, island):
        j0, j1 = anc[c, island, 0], anc[c, island, 1]
        keep = (j0 >= 2).astype(jnp.int32)
        return keep, jnp.where(j0 >= 2, j1, j0), jnp.where(j0 >= 2, j0, j1) - 2

    nxt, prv = (dom + 1) % islands, (dom + islands - 1) % islands
    o0, a0, _ = row_of(0, dom)
    o0p, _, _ = row_of(0, prv)
    _, _, b0n = row_of(0, nxt)
    o1, a1, b1 = row_of(1, dom)
    _, _, b1n = row_of(1, nxt)

    @pl.when(lat < lats - 1)
    def _():
        for c in halo(0):
            c.wait_recv()

    @pl.when(lat > 0)
    def _():
        for c in halo(1):
            c.wait_recv()

    def masked(t, val):
        if t == 1:
            return jnp.where(lat > 0, val, 0.0)
        if t == 4:
            return jnp.where(lat < lats - 1, val, 0.0)
        return val

    def forecast():
        def step(_, carry):
            for src, dst, old in ((a, b, None), (b, a, a)):
                for t in range(1, 5):
                    new = stage_tile(src, old, cor, t)
                    for f in range(3):
                        dst[f, pl.ds(8 * t, 8), :] = masked(t, new[f])
            return carry

        lax.fori_loop(0, 2, step, 0)

    def twice(pick):
        for t in range(1, 5):
            r = 8 * t
            for f in range(3):
                a[f, pl.ds(r, 8), :] = jnp.where(
                    pick == 1, xe[f, 1, pl.ds(r - 8, 8), :], xe[f, 0, pl.ds(r - 8, 8), :]
                )
        forecast()
        for t in range(1, 5):
            r = 8 * t
            add = jnp.where(pick == 1, ne[1, pl.ds(r - 8, 8), :], ne[0, pl.ds(r - 8, 8), :])
            a[0, pl.ds(r, 8), :] = masked(t, a[0, pl.ds(r, 8), :] + add)
        forecast()

    def send(d, n, k):
        src = own.at[d, k] if n == 1 else ring.at[d, n - 2, k]
        return pltpu.make_async_remote_copy(
            src, ring.at[d, n - 1, k], rsend.at[d, n - 1, k], rrecv.at[d, n - 1, k],
            device_id=hop(d, n), device_id_type=MESH,
        )

    def pass_on(d):
        return pltpu.make_async_remote_copy(
            own.at[d, pl.ds(0, 3)], byp.at[d], bsend.at[d], brecv.at[d],
            device_id=at(nxt_xy, z), device_id_type=MESH,
        )

    twice(b0n)
    for f in range(3):
        for d in range(2):
            own[d, f] = a[f, pl.ds(16 + 8 * d, 8), :]
            send(d, 1, f).start()
    for d in range(2):
        pass_on(d).start()

    twice(a0)
    for d in range(2):
        rows = pl.ds(8 * d, 8)
        fh = a[0, pl.ds(16 + 8 * d, 8), :]
        foh[d] = fh
        own[d, 3] = jnp.where(b1n == o0, fh, 0.0) + jnp.where(b1n == 1, n1[1, rows, :], n1[0, rows, :])
        send(d, 1, 3).start()
    for f in range(1, 3):
        for d in range(2):
            own[d, 3 + f] = a[f, pl.ds(16 + 8 * d, 8), :]
            send(d, 1, 3 + f).start()

    for n in range(2, HOPS + 1):
        for k in range(6):
            for d in range(2):
                send(d, n - 1, k).wait_recv()
                send(d, n, k).start()

    @pl.when(lat > 0)
    def _():
        for c in halo(0):
            c.wait_send()

    @pl.when(lat < lats - 1)
    def _():
        for c in halo(1):
            c.wait_send()

    for d in range(2):
        pass_on(d).wait()
    for n in range(1, HOPS):
        for k in range(6):
            for d in range(2):
                send(d, n, k).wait_send()

    last = HOPS - 1

    def put(f, d, va, vb):
        rows = pl.ds(8 * d, 8)
        ovm[f, 0, rows, :] = jnp.where(o1 == 0, va, vb)
        ovm[f, 1, rows, :] = jnp.where(o1 == 0, vb, va)

    for k in range(3):
        for d in range(2):
            send(d, HOPS, k).wait_recv()
    for f in range(3):
        for d in range(2):
            rows = pl.ds(8 * d, 8)
            mine = foh[d] if f == 0 else own[d, 3 + f]
            va = jnp.where(a1 == o0, mine, ring[d, last, f])
            if f == 0:
                va = va + jnp.where(a1 == 1, n1[1, rows, :], n1[0, rows, :])
            send(d, HOPS, 3 + f).wait_recv()
            arrived = ring[d, last, 3 + f]
            if f == 0:
                vb = arrived + jnp.where(b1 == o0p, 0.0, byp[d, 0])
            else:
                vb = jnp.where(b1 == o0p, arrived, byp[d, f])
            put(f, d, va, vb)
        pltpu.make_async_copy(ovm.at[f], out.at[f], osem.at[f]).start()
    for k in range(6):
        for d in range(2):
            send(d, HOPS, k).wait_send()
    for f in range(3):
        pltpu.make_async_copy(ovm.at[f], out.at[f], osem.at[f]).wait()


def solution(mesh):
    islands, lats = mesh.shape["dom"], mesh.shape["lat"]

    def body(states, stir_noise, ancestors):
        f32 = jnp.float32
        dma = pltpu.SemaphoreType.DMA
        return pl.pallas_call(
            functools.partial(kernel, islands, lats),
            out_shape=jax.ShapeDtypeStruct(states.shape, f32),
            in_specs=[
                pl.BlockSpec(memory_space=pltpu.SMEM),
                pl.BlockSpec(memory_space=pl.ANY),
                pl.BlockSpec(memory_space=pl.ANY),
            ],
            out_specs=pl.BlockSpec(memory_space=pl.ANY),
            scratch_shapes=[
                pltpu.VMEM((3, 2, 32, W), f32),
                pltpu.VMEM((2, 32, W), f32),
                pltpu.VMEM((2, 16, W), f32),
                pltpu.VMEM((3, 48, W), f32),
                pltpu.VMEM((3, 48, W), f32),
                pltpu.VMEM((48, 128), f32),
                pltpu.VMEM((2, 6, 8, W), f32),
                pltpu.VMEM((2, 8, W), f32),
                pltpu.VMEM((2, HOPS, 6, 8, W), f32),
                pltpu.VMEM((2, 3, 8, W), f32),
                pltpu.VMEM((3, 2, 16, W), f32),
                dma((3,)),
                dma((2, 2)),
                dma((2, 2)),
                dma((2, HOPS, 6)),
                dma((2, HOPS, 6)),
                dma((2,)),
                dma((2,)),
                dma((3,)),
            ],
            compiler_params=pltpu.CompilerParams(collective_id=0, has_side_effects=True),
            name="filter_ring",
        )(ancestors, states, stir_noise)

    spec = P(None, "dom", "lat", None)
    return jax.shard_map(body, mesh=mesh, in_specs=(spec, spec, P()), out_specs=spec, check_vma=False)
```

time: 178 us -> 67.8 us (0.38)
  the two profiles are of different devices: /device:TPU:103 before, /device:TPU:1 now
where the time goes in v1:
time: 67.8 us; the launch traced here: 67.5 us
  Pallas kernels  64.4 us (95%)
  local copies, waits for them, and re-layouts  3.15 us (5%)
    pallas_call x1, Pallas kernels, body(): pl.pallas_call(functools.partial(kernel, islands, lats), out_shape=jax.Sh...  64.4 us
    unnamed x2, local copies, waits for them, and re-layouts  3.15 us

profile of v1, /device:TPU:1, one launch (start us, length us, event | category | flops | bytes accessed | tf_op | source)
XLA Modules:
  0.0 67.5 jit_solution(8705829324170406189)
XLA Ops:
  0.0 1.4 %copy.4.anc = s32[2,32,2]{2,1,0:T(8,128)} copy(s32[2,32,2]{1,2,0:T(2,128)} %param.5) | data formatting | bytes 1024 | tf_op args[2]
  1.4 64.4 %filter_ring.1 = f32[3,2,16,1024]{3,2,1,0:T(8,128)} custom-call(s32[2,32,2]{2,1,0:T(8,128)} %copy.4.anc, f32[3,2,16,1024]{3,2,1,0:T(8,128)} %states.1, f32[2,2,16,1024]{3,2,1,0:T(8,128)} %noise.1), custom_call_target="tpu_custom_call" | custom-call | tf_op jit(solution)/shard_map/filter_ring/pallas_call | solution.py:301
  65.8 1.8 %copy.6 = f32[3,2,16,1024]{3,2,1,0:T(8,128)} copy(f32[3,2,16,1024]{3,2,1,0:T(8,128)} %filter_ring.1) | data formatting | bytes 786432

commit v2 on v1

--- a/solution.py
+++ b/solution.py
@@ -14,6 +14,7 @@
 ROT = 0.3
 W = 1024
 HOPS = 8
+SIDE = 4
 
 
 def terms(h, u, v, hs, us, vs, cor):
@@ -61,8 +62,8 @@
 
 
 def kernel(
-    islands, lats, anc, states, noise, out, xe, ne, n1, a, b, cor, own, foh, ring, byp, ovm,
-    lsem, hsend, hrecv, rsend, rrecv, bsend, brecv, osem,
+    islands, lats, parents, states, noise, out, anc, xr, n0, xs, n1, a, b, cor, own, foh, ring, byp,
+    lsem, hsend, hrecv, rsend, rrecv, bsend, brecv,
 ):
     dom, lat = lax.axis_index("dom"), lax.axis_index("lat")
     columns = islands // 2
@@ -76,27 +77,37 @@
 
     zs = ((z + 1) % depth, (z + depth - 1) % depth)
     nxt_xy, prv_xy = (xy + 1) % columns, (xy + columns - 1) % columns
-    low = (z < half).astype(jnp.int32)
+    side = SIDE
+    x, y = xy // side, xy % side
+    east = x * side + (y + 1) % side
+    west = x * side + (y + side - 1) % side
+    over = (xy + side) % columns
+    under = (xy + columns - side) % columns
 
     def hop(d, n):
-        zt = zs[d]
-        if n < HOPS:
-            return at(xy, zt)
-        return at((xy + (zt < half).astype(jnp.int32)) % columns, zt)
+        origin = (z + depth - (n - 1)) % depth if d == 0 else (z + n - 1) % depth
+        high = origin // half
+        to = xy
+        if n == 3:
+            to = high * east + (1 - high) * xy
+        if n == 5:
+            wrap = high * (y == 0).astype(jnp.int32)
+            to = wrap * over + (1 - wrap) * xy
+        return at(to, zs[d])
 
     loads = [
-        pltpu.make_async_copy(states, xe.at[:, :, pl.ds(8, 16)], lsem.at[0]),
-        pltpu.make_async_copy(noise.at[0], ne.at[:, pl.ds(8, 16)], lsem.at[1]),
+        pltpu.make_async_copy(states, xr, lsem.at[0]),
+        pltpu.make_async_copy(noise.at[0], n0, lsem.at[1]),
         pltpu.make_async_copy(noise.at[1], n1, lsem.at[2]),
+        pltpu.make_async_copy(parents, anc, lsem.at[3]),
     ]
     for c in loads:
         c.start()
 
     barrier = pltpu.get_barrier_semaphore()
-    from_xy = (xy + columns - low) % columns
     for d in range(2):
-        pl.semaphore_signal(barrier, 1, device_id=at(xy, zs[d]), device_id_type=MESH)
-        pl.semaphore_signal(barrier, 1, device_id=at(from_xy, zs[d]), device_id_type=MESH)
+        for col in (xy, west, under):
+            pl.semaphore_signal(barrier, 1, device_id=at(col, zs[d]), device_id_type=MESH)
     pl.semaphore_signal(barrier, 1, device_id=at(prv_xy, z), device_id_type=MESH)
 
     @pl.when(lat > 0)
@@ -112,46 +123,16 @@
 
     @pl.when(lat == 0)
     def _():
-        xe[:, :, pl.ds(0, 8), :] = jnp.zeros((3, 2, 8, W), jnp.float32)
-        ne[:, pl.ds(0, 8), :] = jnp.zeros((2, 8, W), jnp.float32)
+        xs[:, :, pl.ds(0, 8), :] = jnp.zeros((2, 4, 8, W), jnp.float32)
 
     @pl.when(lat == lats - 1)
     def _():
-        xe[:, :, pl.ds(24, 8), :] = jnp.zeros((3, 2, 8, W), jnp.float32)
-        ne[:, pl.ds(24, 8), :] = jnp.zeros((2, 8, W), jnp.float32)
+        xs[:, :, pl.ds(24, 8), :] = jnp.zeros((2, 4, 8, W), jnp.float32)
 
     for c in loads:
         c.wait()
-    pl.semaphore_wait(
-        barrier, 5 + (lat > 0).astype(jnp.int32) + (lat < lats - 1).astype(jnp.int32)
-    )
-
-    def halo(d):
-        s, t = (8, 24) if d == 0 else (16, 0)
-        dev = (dom, lat - 1) if d == 0 else (dom, lat + 1)
-        return [
-            pltpu.make_async_remote_copy(
-                xe.at[:, :, pl.ds(s, 8)], xe.at[:, :, pl.ds(t, 8)], hsend.at[d, 0], hrecv.at[d, 0],
-                device_id=dev, device_id_type=MESH,
-            ),
-            pltpu.make_async_remote_copy(
-                ne.at[:, pl.ds(s, 8)], ne.at[:, pl.ds(t, 8)], hsend.at[d, 1], hrecv.at[d, 1],
-                device_id=dev, device_id_type=MESH,
-            ),
-        ]
-
-    @pl.when(lat > 0)
-    def _():
-        for c in halo(0):
-            c.start()
-
-    @pl.when(lat < lats - 1)
-    def _():
-        for c in halo(1):
-            c.start()
-
     def row_of(c, island):
-        j0, j1 = anc[c, island, 0], anc[c, island, 1]
+        j0, j1 = anc[c, 0, island], anc[c, 1, island]
         keep = (j0 >= 2).astype(jnp.int32)
         return keep, jnp.where(j0 >= 2, j1, j0), jnp.where(j0 >= 2, j0, j1) - 2
 
@@ -162,15 +143,45 @@
     o1, a1, b1 = row_of(1, dom)
     _, _, b1n = row_of(1, nxt)
 
-    @pl.when(lat < lats - 1)
-    def _():
-        for c in halo(0):
-            c.wait_recv()
-
-    @pl.when(lat > 0)
-    def _():
-        for c in halo(1):
-            c.wait_recv()
+    def choose(p, pick, rows):
+        for f in range(3):
+            xs[p, f, pl.ds(8 + rows, 8), :] = jnp.where(
+                pick == 1, xr[f, 1, pl.ds(rows, 8), :], xr[f, 0, pl.ds(rows, 8), :]
+            )
+        xs[p, 3, pl.ds(8 + rows, 8), :] = jnp.where(pick == 1, n0[1, pl.ds(rows, 8), :], n0[0, pl.ds(rows, 8), :])
+
+    for p, pick in ((0, b0n), (1, a0)):
+        for rows in (0, 8):
+            choose(p, pick, rows)
+
+    pl.semaphore_wait(
+        barrier, 7 + (lat > 0).astype(jnp.int32) + (lat < lats - 1).astype(jnp.int32)
+    )
+
+    def halo(d, p):
+        s, t = (8, 24) if d == 0 else (16, 0)
+        return pltpu.make_async_remote_copy(
+            xs.at[p, :, pl.ds(s, 8)], xs.at[p, :, pl.ds(t, 8)], hsend.at[d, p], hrecv.at[d, p],
+            device_id=(dom, lat - 1) if d == 0 else (dom, lat + 1), device_id_type=MESH,
+        )
+
+    for p in range(2):
+        @pl.when(lat > 0)
+        def _():
+            halo(0, p).start()
+
+        @pl.when(lat < lats - 1)
+        def _():
+            halo(1, p).start()
+
+    def arrived_halo(p):
+        @pl.when(lat < lats - 1)
+        def _():
+            halo(0, p).wait_recv()
+
+        @pl.when(lat > 0)
+        def _():
+            halo(1, p).wait_recv()
 
     def masked(t, val):
         if t == 1:
@@ -190,18 +201,16 @@
 
         lax.fori_loop(0, 2, step, 0)
 
-    def twice(pick):
+    def twice(p):
+        arrived_halo(p)
         for t in range(1, 5):
             r = 8 * t
             for f in range(3):
-                a[f, pl.ds(r, 8), :] = jnp.where(
-                    pick == 1, xe[f, 1, pl.ds(r - 8, 8), :], xe[f, 0, pl.ds(r - 8, 8), :]
-                )
+                a[f, pl.ds(r, 8), :] = xs[p, f, pl.ds(r - 8, 8), :]
         forecast()
         for t in range(1, 5):
             r = 8 * t
-            add = jnp.where(pick == 1, ne[1, pl.ds(r - 8, 8), :], ne[0, pl.ds(r - 8, 8), :])
-            a[0, pl.ds(r, 8), :] = masked(t, a[0, pl.ds(r, 8), :] + add)
+            a[0, pl.ds(r, 8), :] = masked(t, a[0, pl.ds(r, 8), :] + xs[p, 3, pl.ds(r - 8, 8), :])
         forecast()
 
     def send(d, n, k):
@@ -217,7 +226,7 @@
             device_id=at(nxt_xy, z), device_id_type=MESH,
         )
 
-    twice(b0n)
+    twice(0)
     for f in range(3):
         for d in range(2):
             own[d, f] = a[f, pl.ds(16 + 8 * d, 8), :]
@@ -225,7 +234,7 @@
     for d in range(2):
         pass_on(d).start()
 
-    twice(a0)
+    twice(1)
     for d in range(2):
         rows = pl.ds(8 * d, 8)
         fh = a[0, pl.ds(16 + 8 * d, 8), :]
@@ -245,13 +254,13 @@
 
     @pl.when(lat > 0)
     def _():
-        for c in halo(0):
-            c.wait_send()
+        for p in range(2):
+            halo(0, p).wait_send()
 
     @pl.when(lat < lats - 1)
     def _():
-        for c in halo(1):
-            c.wait_send()
+        for p in range(2):
+            halo(1, p).wait_send()
 
     for d in range(2):
         pass_on(d).wait()
@@ -264,8 +273,8 @@
 
     def put(f, d, va, vb):
         rows = pl.ds(8 * d, 8)
-        ovm[f, 0, rows, :] = jnp.where(o1 == 0, va, vb)
-        ovm[f, 1, rows, :] = jnp.where(o1 == 0, vb, va)
+        out[f, 0, rows, :] = jnp.where(o1 == 0, va, vb)
+        out[f, 1, rows, :] = jnp.where(o1 == 0, vb, va)
 
     for k in range(3):
         for d in range(2):
@@ -284,12 +293,9 @@
             else:
                 vb = jnp.where(b1 == o0p, arrived, byp[d, f])
             put(f, d, va, vb)
-        pltpu.make_async_copy(ovm.at[f], out.at[f], osem.at[f]).start()
     for k in range(6):
         for d in range(2):
             send(d, HOPS, k).wait_send()
-    for f in range(3):
-        pltpu.make_async_copy(ovm.at[f], out.at[f], osem.at[f]).wait()
 
 
 def solution(mesh):
@@ -302,14 +308,16 @@
             functools.partial(kernel, islands, lats),
             out_shape=jax.ShapeDtypeStruct(states.shape, f32),
             in_specs=[
-                pl.BlockSpec(memory_space=pltpu.SMEM),
-                pl.BlockSpec(memory_space=pl.ANY),
-                pl.BlockSpec(memory_space=pl.ANY),
+                pl.BlockSpec(memory_space=pltpu.HBM),
+                pl.BlockSpec(memory_space=pltpu.HBM),
+                pl.BlockSpec(memory_space=pltpu.HBM),
             ],
-            out_specs=pl.BlockSpec(memory_space=pl.ANY),
+            out_specs=pl.BlockSpec(memory_space=pltpu.VMEM),
             scratch_shapes=[
-                pltpu.VMEM((3, 2, 32, W), f32),
-                pltpu.VMEM((2, 32, W), f32),
+                pltpu.SMEM((2, 2, islands), jnp.int32),
+                pltpu.VMEM((3, 2, 16, W), f32),
+                pltpu.VMEM((2, 16, W), f32),
+                pltpu.VMEM((2, 4, 32, W), f32),
                 pltpu.VMEM((2, 16, W), f32),
                 pltpu.VMEM((3, 48, W), f32),
                 pltpu.VMEM((3, 48, W), f32),
@@ -318,19 +326,17 @@
                 pltpu.VMEM((2, 8, W), f32),
                 pltpu.VMEM((2, HOPS, 6, 8, W), f32),
                 pltpu.VMEM((2, 3, 8, W), f32),
-                pltpu.VMEM((3, 2, 16, W), f32),
-                dma((3,)),
+                dma((4,)),
                 dma((2, 2)),
                 dma((2, 2)),
                 dma((2, HOPS, 6)),
                 dma((2, HOPS, 6)),
                 dma((2,)),
                 dma((2,)),
-                dma((3,)),
             ],
-            compiler_params=pltpu.CompilerParams(collective_id=0, has_side_effects=True),
+            compiler_params=pltpu.CompilerParams(collective_id=0, has_side_effects=True, vmem_limit_bytes=20 * 2**20),
             name="filter_ring",
-        )(ancestors, states, stir_noise)
+        )(*(pltpu.with_memory_space_constraint(v, pltpu.HBM) for v in (jnp.transpose(ancestors, (0, 2, 1)), states, stir_noise)))
 
     spec = P(None, "dom", "lat", None)
     return jax.shard_map(body, mesh=mesh, in_specs=(spec, spec, P()), out_specs=spec, check_vma=False)

time: 67.8 us -> 59.3 us (0.87)
  Pallas kernels: 64.4 us -> 58.4 us
  local copies, waits for them, and re-layouts: 3.15 us -> 0.75 us
    pallas_call x1, Pallas kernels: 64.4 us -> 58.4 us  [body(): pl.pallas_call(functools.partial(kernel, islands, lats), out_shape=jax.Sh...]
    unnamed x2 -> x1, local copies, waits for them, and re-layouts: 3.15 us -> 0.75 us
where the time goes in v2:
time: 59.3 us; the launch traced here: 59.2 us
  Pallas kernels  58.4 us (98%)
  local copies, waits for them, and re-layouts  0.75 us (1%)
    pallas_call x1, Pallas kernels, body(): pl.pallas_call(functools.partial(kernel, islands, lats), out_shape=jax.Sh...  58.4 us

profile of v2, /device:TPU:1, one launch (start us, length us, event | category | flops | bytes accessed | tf_op | source)
XLA Modules:
  0.0 59.2 jit_solution(9867449387576732010)
XLA Ops:
  0.0 58.4 %filter_ring.1 = f32[3,2,16,1024]{3,2,1,0:T(8,128)S(1)} custom-call(s32[2,2,32]{2,1,0:T(2,128)} %bitcast.1, f32[3,2,16,1024]{3,2,1,0:T(8,128)} %states.1, f32[2,2,16,1024]{3,2,1,0:T(8,128)} %noise.1), custom_call_target="tpu_custom_call" | custom-call | tf_op jit(solution)/shard_map/filter_ring/pallas_call | solution.py:307
  58.4 0.7 %copy.5 = f32[3,2,16,1024]{3,2,1,0:T(8,128)} copy(f32[3,2,16,1024]{3,2,1,0:T(8,128)S(1)} %filter_ring.1) | data formatting | bytes 786432

commit v3 on v2

--- a/solution.py
+++ b/solution.py
@@ -11,6 +11,8 @@
 DT = 0.2
 HALF = 0.5 * DT
 NU = 0.05 * DT
+DEPTH = HALF * HALF
+REST = (DEPTH, 0.0, 0.0)
 ROT = 0.3
 W = 1024
 HOPS = 8
@@ -21,19 +23,14 @@
     he, hw, hn, hb = hs
     ue, uw, un, ub = us
     ve, vw, vn, vb = vs
-    dux = ue - uw
-    dvy = vn - vb
-    bh = (he * ue - hw * uw) + (hn * vn - hb * vb) + (dux + dvy)
-    bu = u * dux + v * (un - ub) + (he - hw)
-    bv = u * (ve - vw) + v * dvy + (hn - hb)
+    keep = 1.0 - 4.0 * NU
     lh = (he + hw) + (hn + hb)
     lu = (ue + uw) + (un + ub)
     lv = (ve + vw) + (vn + vb)
-    keep = 1.0 - 4.0 * NU
     return (
-        h * keep + NU * lh - HALF * bh,
-        u * keep + NU * lu - HALF * bu + cor * v,
-        v * keep + NU * lv - HALF * bv - cor * u,
+        h * keep + NU * lh - ((he * ue - hw * uw) + (hn * vn - hb * vb)),
+        u * (keep - (ue - uw)) + v * (cor - (un - ub)) + (NU * lu - (he - hw)),
+        v * (keep - (vn - vb)) - u * (cor + (ve - vw)) + (NU * lv - (hn - hb)),
     )
 
 
@@ -50,8 +47,8 @@
             (
                 pltpu.roll(c, W - 1, 1),
                 pltpu.roll(c, 1, 1),
-                jnp.where(sub == 7, pltpu.roll(nxt, 7, 0), pltpu.roll(c, 7, 0)),
-                jnp.where(sub == 0, pltpu.roll(prv, 1, 0), pltpu.roll(c, 1, 0)),
+                pltpu.roll(jnp.where(sub == 0, nxt, c), 7, 0),
+                pltpu.roll(jnp.where(sub == 7, prv, c), 1, 0),
             )
         )
     cr = jnp.broadcast_to(cor[pl.ds(r, 8), 0:1], (8, W))
@@ -124,10 +121,12 @@
     @pl.when(lat == 0)
     def _():
         xs[:, :, pl.ds(0, 8), :] = jnp.zeros((2, 4, 8, W), jnp.float32)
+        xs[:, 0, pl.ds(0, 8), :] = jnp.full((2, 8, W), DEPTH, jnp.float32)
 
     @pl.when(lat == lats - 1)
     def _():
         xs[:, :, pl.ds(24, 8), :] = jnp.zeros((2, 4, 8, W), jnp.float32)
+        xs[:, 0, pl.ds(24, 8), :] = jnp.full((2, 8, W), DEPTH, jnp.float32)
 
     for c in loads:
         c.wait()
@@ -145,10 +144,10 @@
 
     def choose(p, pick, rows):
         for f in range(3):
-            xs[p, f, pl.ds(8 + rows, 8), :] = jnp.where(
-                pick == 1, xr[f, 1, pl.ds(rows, 8), :], xr[f, 0, pl.ds(rows, 8), :]
-            )
-        xs[p, 3, pl.ds(8 + rows, 8), :] = jnp.where(pick == 1, n0[1, pl.ds(rows, 8), :], n0[0, pl.ds(rows, 8), :])
+            raw = jnp.where(pick == 1, xr[f, 1, pl.ds(rows, 8), :], xr[f, 0, pl.ds(rows, 8), :])
+            xs[p, f, pl.ds(8 + rows, 8), :] = raw * HALF if f else DEPTH + raw * DEPTH
+        add = jnp.where(pick == 1, n0[1, pl.ds(rows, 8), :], n0[0, pl.ds(rows, 8), :])
+        xs[p, 3, pl.ds(8 + rows, 8), :] = add * DEPTH
 
     for p, pick in ((0, b0n), (1, a0)):
         for rows in (0, 8):
@@ -183,23 +182,25 @@
         def _():
             halo(1, p).wait_recv()
 
-    def masked(t, val):
+    def masked(t, val, f):
         if t == 1:
-            return jnp.where(lat > 0, val, 0.0)
+            return jnp.where(lat > 0, val, REST[f])
         if t == 4:
-            return jnp.where(lat < lats - 1, val, 0.0)
+            return jnp.where(lat < lats - 1, val, REST[f])
         return val
 
-    def forecast():
-        def step(_, carry):
-            for src, dst, old in ((a, b, None), (b, a, a)):
-                for t in range(1, 5):
-                    new = stage_tile(src, old, cor, t)
-                    for f in range(3):
-                        dst[f, pl.ds(8 * t, 8), :] = masked(t, new[f])
-            return carry
-
-        lax.fori_loop(0, 2, step, 0)
+    def section(src, dst, old, tiles):
+        for t in tiles:
+            new = stage_tile(src, old, cor, t)
+            for f in range(3):
+                dst[f, pl.ds(8 * t, 8), :] = masked(t, new[f], f)
+
+    def forecast(last):
+        every = range(1, 5)
+        section(a, b, None, every)
+        section(b, a, a, every)
+        section(a, b, None, every)
+        section(b, a, a, range(2, 4) if last else every)
 
     def twice(p):
         arrived_halo(p)
@@ -207,11 +208,11 @@
             r = 8 * t
             for f in range(3):
                 a[f, pl.ds(r, 8), :] = xs[p, f, pl.ds(r - 8, 8), :]
-        forecast()
+        forecast(False)
         for t in range(1, 5):
             r = 8 * t
-            a[0, pl.ds(r, 8), :] = masked(t, a[0, pl.ds(r, 8), :] + xs[p, 3, pl.ds(r - 8, 8), :])
-        forecast()
+            a[0, pl.ds(r, 8), :] = masked(t, a[0, pl.ds(r, 8), :] + xs[p, 3, pl.ds(r - 8, 8), :], 0)
+        forecast(True)
 
     def send(d, n, k):
         src = own.at[d, k] if n == 1 else ring.at[d, n - 2, k]
@@ -239,7 +240,7 @@
         rows = pl.ds(8 * d, 8)
         fh = a[0, pl.ds(16 + 8 * d, 8), :]
         foh[d] = fh
-        own[d, 3] = jnp.where(b1n == o0, fh, 0.0) + jnp.where(b1n == 1, n1[1, rows, :], n1[0, rows, :])
+        own[d, 3] = jnp.where(b1n == o0, fh, 0.0) + DEPTH * jnp.where(b1n == 1, n1[1, rows, :], n1[0, rows, :])
         send(d, 1, 3).start()
     for f in range(1, 3):
         for d in range(2):
@@ -271,6 +272,9 @@
 
     last = HOPS - 1
 
+    def plain(f, v):
+        return v * (1.0 / HALF) if f else v * (1.0 / DEPTH) - 1.0
+
     def put(f, d, va, vb):
         rows = pl.ds(8 * d, 8)
         out[f, 0, rows, :] = jnp.where(o1 == 0, va, vb)
@@ -285,14 +289,14 @@
             mine = foh[d] if f == 0 else own[d, 3 + f]
             va = jnp.where(a1 == o0, mine, ring[d, last, f])
             if f == 0:
-                va = va + jnp.where(a1 == 1, n1[1, rows, :], n1[0, rows, :])
+                va = va + DEPTH * jnp.where(a1 == 1, n1[1, rows, :], n1[0, rows, :])
             send(d, HOPS, 3 + f).wait_recv()
             arrived = ring[d, last, 3 + f]
             if f == 0:
                 vb = arrived + jnp.where(b1 == o0p, 0.0, byp[d, 0])
             else:
                 vb = jnp.where(b1 == o0p, arrived, byp[d, f])
-            put(f, d, va, vb)
+            put(f, d, plain(f, va), plain(f, vb))
     for k in range(6):
         for d in range(2):
             send(d, HOPS, k).wait_send()

time: 59.3 us -> 57.9 us (0.976)
  Pallas kernels: 58.4 us -> 56.7 us
    pallas_call x1, Pallas kernels: 58.4 us -> 56.7 us  [body(): pl.pallas_call(functools.partial(kernel, islands, lats), out_shape=jax.Sh...]
where the time goes in v3:
time: 57.9 us; the launch traced here: 57.4 us
  Pallas kernels  56.7 us (98%)
  local copies, waits for them, and re-layouts  0.75 us (1%)
    pallas_call x1, Pallas kernels, body(): pl.pallas_call(functools.partial(kernel, islands, lats), out_shape=jax.Sh...  56.7 us

profile of v3, /device:TPU:1, one launch (start us, length us, event | category | flops | bytes accessed | tf_op | source)
XLA Modules:
  0.0 57.4 jit_solution(7904893272537682598)
XLA Ops:
  0.0 56.7 %filter_ring.1 = f32[3,2,16,1024]{3,2,1,0:T(8,128)S(1)} custom-call(s32[2,2,32]{2,1,0:T(2,128)} %bitcast.1, f32[3,2,16,1024]{3,2,1,0:T(8,128)} %states.1, f32[2,2,16,1024]{3,2,1,0:T(8,128)} %noise.1), custom_call_target="tpu_custom_call" | custom-call | tf_op jit(solution)/shard_map/filter_ring/pallas_call | solution.py:311
  56.7 0.7 %copy.5 = f32[3,2,16,1024]{3,2,1,0:T(8,128)} copy(f32[3,2,16,1024]{3,2,1,0:T(8,128)S(1)} %filter_ring.1) | data formatting | bytes 786432

commit v4 on v3

--- a/solution.py
+++ b/solution.py
@@ -85,9 +85,9 @@
         origin = (z + depth - (n - 1)) % depth if d == 0 else (z + n - 1) % depth
         high = origin // half
         to = xy
-        if n == 3:
+        if n == 4:
             to = high * east + (1 - high) * xy
-        if n == 5:
+        if n == 6:
             wrap = high * (y == 0).astype(jnp.int32)
             to = wrap * over + (1 - wrap) * xy
         return at(to, zs[d])

time: 57.9 us -> 57 us (0.984)
  Pallas kernels: 56.7 us -> 56.1 us
    pallas_call x1, Pallas kernels: 56.7 us -> 56.1 us  [body(): pl.pallas_call(functools.partial(kernel, islands, lats), out_shape=jax.Sh...]
where the time goes in v4:
time: 57 us; the launch traced here: 56.8 us
  Pallas kernels  56.1 us (98%)
  local copies, waits for them, and re-layouts  0.75 us (1%)
    pallas_call x1, Pallas kernels, body(): pl.pallas_call(functools.partial(kernel, islands, lats), out_shape=jax.Sh...  56.1 us

profile of v4, /device:TPU:1, one launch (start us, length us, event | category | flops | bytes accessed | tf_op | source)
XLA Modules:
  0.0 56.8 jit_solution(2033994199216757980)
XLA Ops:
  0.0 56.1 %filter_ring.1 = f32[3,2,16,1024]{3,2,1,0:T(8,128)S(1)} custom-call(s32[2,2,32]{2,1,0:T(2,128)} %bitcast.1, f32[3,2,16,1024]{3,2,1,0:T(8,128)} %states.1, f32[2,2,16,1024]{3,2,1,0:T(8,128)} %noise.1), custom_call_target="tpu_custom_call" | custom-call | tf_op jit(solution)/shard_map/filter_ring/pallas_call | solution.py:311
  56.1 0.7 %copy.5 = f32[3,2,16,1024]{3,2,1,0:T(8,128)} copy(f32[3,2,16,1024]{3,2,1,0:T(8,128)S(1)} %filter_ring.1) | data formatting | bytes 786432

commit v5 on v4

--- a/solution.py
+++ b/solution.py
@@ -87,7 +87,7 @@
         to = xy
         if n == 4:
             to = high * east + (1 - high) * xy
-        if n == 6:
+        if n == 5:
             wrap = high * (y == 0).astype(jnp.int32)
             to = wrap * over + (1 - wrap) * xy
         return at(to, zs[d])
@@ -103,8 +103,14 @@
 
     barrier = pltpu.get_barrier_semaphore()
     for d in range(2):
-        for col in (xy, west, under):
+        for col in (xy, west):
             pl.semaphore_signal(barrier, 1, device_id=at(col, zs[d]), device_id_type=MESH)
+
+    @pl.when(y == 0)
+    def _():
+        for d in range(2):
+            pl.semaphore_signal(barrier, 1, device_id=at(under, zs[d]), device_id_type=MESH)
+
     pl.semaphore_signal(barrier, 1, device_id=at(prv_xy, z), device_id_type=MESH)
 
     @pl.when(lat > 0)
@@ -154,7 +160,7 @@
             choose(p, pick, rows)
 
     pl.semaphore_wait(
-        barrier, 7 + (lat > 0).astype(jnp.int32) + (lat < lats - 1).astype(jnp.int32)
+        barrier, 5 + 2 * (y == 0).astype(jnp.int32) + (lat > 0).astype(jnp.int32) + (lat < lats - 1).astype(jnp.int32)
     )
 
     def halo(d, p):
@@ -195,24 +201,28 @@
             for f in range(3):
                 dst[f, pl.ds(8 * t, 8), :] = masked(t, new[f], f)
 
-    def forecast(last):
+    def forecast(emit=None):
         every = range(1, 5)
         section(a, b, None, every)
         section(b, a, a, every)
         section(a, b, None, every)
-        section(b, a, a, range(2, 4) if last else every)
-
-    def twice(p):
+        if emit is None:
+            section(b, a, a, every)
+        else:
+            for d in range(2):
+                emit(d, stage_tile(b, a, cor, 2 + d))
+
+    def twice(p, emit):
         arrived_halo(p)
         for t in range(1, 5):
             r = 8 * t
             for f in range(3):
                 a[f, pl.ds(r, 8), :] = xs[p, f, pl.ds(r - 8, 8), :]
-        forecast(False)
+        forecast()
         for t in range(1, 5):
             r = 8 * t
             a[0, pl.ds(r, 8), :] = masked(t, a[0, pl.ds(r, 8), :] + xs[p, 3, pl.ds(r - 8, 8), :], 0)
-        forecast(True)
+        forecast(emit)
 
     def send(d, n, k):
         src = own.at[d, k] if n == 1 else ring.at[d, n - 2, k]
@@ -227,25 +237,24 @@
             device_id=at(nxt_xy, z), device_id_type=MESH,
         )
 
-    twice(0)
-    for f in range(3):
-        for d in range(2):
-            own[d, f] = a[f, pl.ds(16 + 8 * d, 8), :]
+    def emit_first(d, new):
+        for f in range(3):
+            own[d, f] = new[f]
             send(d, 1, f).start()
+
+    def emit_second(d, new):
+        rows = pl.ds(8 * d, 8)
+        foh[d] = new[0]
+        own[d, 3] = jnp.where(b1n == o0, new[0], 0.0) + DEPTH * jnp.where(b1n == 1, n1[1, rows, :], n1[0, rows, :])
+        own[d, 4] = new[1]
+        own[d, 5] = new[2]
+        for k in range(3, 6):
+            send(d, 1, k).start()
+
+    twice(0, emit_first)
     for d in range(2):
         pass_on(d).start()
-
-    twice(1)
-    for d in range(2):
-        rows = pl.ds(8 * d, 8)
-        fh = a[0, pl.ds(16 + 8 * d, 8), :]
-        foh[d] = fh
-        own[d, 3] = jnp.where(b1n == o0, fh, 0.0) + DEPTH * jnp.where(b1n == 1, n1[1, rows, :], n1[0, rows, :])
-        send(d, 1, 3).start()
-    for f in range(1, 3):
-        for d in range(2):
-            own[d, 3 + f] = a[f, pl.ds(16 + 8 * d, 8), :]
-            send(d, 1, 3 + f).start()
+    twice(1, emit_second)
 
     for n in range(2, HOPS + 1):
         for k in range(6):

time: 57 us -> 56.9 us (level)
  no operation moved by 1% of the time
where the time goes in v5:
time: 56.9 us; the launch traced here: 56.8 us
  Pallas kernels  56 us (98%)
  local copies, waits for them, and re-layouts  0.75 us (1%)
    pallas_call x1, Pallas kernels, body(): pl.pallas_call(functools.partial(kernel, islands, lats), out_shape=jax.Sh...  56 us

profile of v5, /device:TPU:1, one launch (start us, length us, event | category | flops | bytes accessed | tf_op | source)
XLA Modules:
  0.0 56.8 jit_solution(14511281275778944566)
XLA Ops:
  0.0 56.0 %filter_ring.1 = f32[3,2,16,1024]{3,2,1,0:T(8,128)S(1)} custom-call(s32[2,2,32]{2,1,0:T(2,128)} %bitcast.1, f32[3,2,16,1024]{3,2,1,0:T(8,128)} %states.1, f32[2,2,16,1024]{3,2,1,0:T(8,128)} %noise.1), custom_call_target="tpu_custom_call" | custom-call | tf_op jit(solution)/shard_map/filter_ring/pallas_call | solution.py:320
  56.0 0.7 %copy.5 = f32[3,2,16,1024]{3,2,1,0:T(8,128)} copy(f32[3,2,16,1024]{3,2,1,0:T(8,128)S(1)} %filter_ring.1) | data formatting | bytes 786432
